TPU v7x, 32 devices: a whole 2x2x4 slice. The times are simulated.
32 devices in a mesh: seq: 8 (over z, y), head: 4 (over x, core).
Axes of the slice: x: 2, y: 2, z: 4, core: 2. Of those that a mesh axis runs over, the one named last changes fastest.
Arguments:
- queries: bfloat16 [4096, 1024], P('seq', 'head'), may hold values from -6 to 6
- keys: bfloat16 [4096, 1024], P('seq', 'head'), may hold values from -6 to 6
- values: bfloat16 [4096, 1024], P('seq', 'head'), may hold values from -4 to 4
- masked: int32 [4096], P('seq'), may hold values from 0 to 1
- mask_qkv: bfloat16 [3, 1024], P(None, 'head'), may hold values from -5.09375 to 5.09375
- key_bars: int32 [32, 4], P('seq'), may hold values from -1 to 31, as said below
- w_out: bfloat16 [1024, 1536], P('head'), may hold values from -0.1875 to 0.1875
Outputs:
- attn_out: bfloat16 [4096, 1536], P('seq', 'head')
Inputs may be any that keep to these rules, and one draw needn't show every extreme that they name: `key_bars`: entry [b, s] is -1 or a bar on the device s - 2 places along seq for s < 2, s - 1 places for s >= 2. Bar b lists bar a in slot s exactly when a lists b in slot 3 - s. No listed bar is b or next to b. The bars of one device list at most 2 bars of any one other device, and some pair of devices reaches 2.
All inputs are finite; a program needn't handle non-finite values.
Results may differ from a plain program's by a relative error of at most 0.009.
Values may be sent and summed in bfloat16 or wider, within the bound.
A program may use at most 64 MiB of HBM per device.

v0:
```python
import math

import jax
import jax.numpy as jnp
from jax import lax
from jax.sharding import PartitionSpec as P

HD = 64
R = 2


def shifted(block, axis, distance):
    devices = range(lax.axis_size(axis))
    route = [(i - distance, i) for i in devices if i - distance in devices]
    return lax.ppermute(block, axis, route)


def attend_group(inputs):
    query_grp, block_grp, usable = inputs
    head_count = query_grp.shape[2]
    feat_width = head_count * HD
    shaped = (block_grp.shape[0], block_grp.shape[1], block_grp.shape[2], head_count, HD)
    key_grp = block_grp[..., :feat_width].reshape(shaped)
    value_grp = block_grp[..., feat_width:].reshape(shaped)
    scaling = 1.0 / math.sqrt(HD)
    scores = (
        jnp.einsum("gqhd,gnkhd->ghqnk", query_grp, key_grp, preferred_element_type=jnp.float32)
        * scaling
    )
    scores = jnp.where(usable[:, None, None, :, None], scores, -jnp.inf)
    row_max = jnp.max(scores, axis=(3, 4), keepdims=True)
    raised = jnp.exp(scores - row_max)
    totals = jnp.sum(raised, axis=(3, 4))
    rounded = raised.astype(jnp.bfloat16)
    weighted = jnp.einsum(
        "ghqnk,gnkhd->gqhd", rounded, value_grp, preferred_element_type=jnp.float32
    )
    return (weighted / jnp.transpose(totals, (0, 2, 1))[..., None]).astype(jnp.bfloat16)


def on_device(queries, keys, values, masked, mask_qkv, key_bars, w_out):
    local_tokens, feat_width = queries.shape
    bar_count = key_bars.shape[0]
    bar_len = local_tokens // bar_count
    head_count = feat_width // HD
    flagged = (masked == 1)[:, None]
    query_eff = jnp.where(flagged, mask_qkv[0][None, :], queries)
    key_eff = jnp.where(flagged, mask_qkv[1][None, :], keys)
    value_eff = jnp.where(flagged, mask_qkv[2][None, :], values)
    paired = jnp.concatenate([key_eff, value_eff], axis=1).reshape(
        bar_count, bar_len, 2 * feat_width
    )
    my_index = lax.axis_index("seq")
    seq_count = lax.axis_size("seq")
    local_ids = jnp.arange(bar_count, dtype=jnp.int32)
    global_bar = my_index * bar_count + local_ids
    chosen_list = []
    for column in range(2 * R):
        offset = column - R if column < R else column - R + 1
        remote = shifted(paired, "seq", -offset)
        wanted = key_bars[:, column]
        picker = (jnp.remainder(wanted, bar_count)[:, None] == local_ids[None, :]).astype(
            jnp.bfloat16
        )
        chosen_list.append(
            jnp.einsum("lj,jkf->lkf", picker, remote, preferred_element_type=jnp.float32).astype(
                jnp.bfloat16
            )
        )
        if offset == -1:
            rim_low = remote[bar_count - 1]
        if offset == 1:
            rim_high = remote[0]
    previous = jnp.concatenate([rim_low[None], paired[:-1]], axis=0)
    following = jnp.concatenate([paired[1:], rim_high[None]], axis=0)
    blocks = jnp.stack([previous, paired, following] + chosen_list, axis=1)
    band_usable = [global_bar > 0, global_bar >= 0, global_bar < bar_count * seq_count - 1]
    usable = jnp.stack(band_usable + [key_bars[:, column] >= 0 for column in range(2 * R)], axis=1)
    group_size = bar_count
    while group_size * bar_len > 512 and group_size % 2 == 0:
        group_size = group_size // 2
    steps_num = bar_count // group_size
    query_shaped = query_eff.reshape(steps_num, group_size, bar_len, head_count, HD)
    block_shaped = blocks.reshape((steps_num, group_size) + blocks.shape[1:])
    usable_shaped = usable.reshape(steps_num, group_size, usable.shape[1])
    attended = lax.map(attend_group, (query_shaped, block_shaped, usable_shaped))
    attended = attended.reshape(local_tokens, feat_width)
    head_group = lax.axis_size("head")
    col_width = w_out.shape[1] // head_group
    all_heads = lax.all_gather(attended, "head", axis=1, tiled=True)
    all_rows = lax.all_to_all(w_out, "head", split_axis=1, concat_axis=0, tiled=True)
    summed = jnp.zeros((local_tokens, col_width), jnp.float32)
    for member in range(head_group):
        term = jnp.dot(
            all_heads[:, member * feat_width : (member + 1) * feat_width],
            all_rows[member * feat_width : (member + 1) * feat_width],
            preferred_element_type=jnp.float32,
        )
        summed = summed + lax.optimization_barrier(term.astype(jnp.bfloat16)).astype(jnp.float32)
    return summed.astype(jnp.bfloat16)


def solution(mesh):
    placed = (
        P("seq", "head"),
        P("seq", "head"),
        P("seq", "head"),
        P("seq"),
        P(None, "head"),
        P("seq", None),
        P("head", None),
    )
    return jax.shard_map(
        on_device, mesh=mesh, in_specs=placed, out_specs=P("seq", "head"), check_vma=False
    )
```

profile of v0, /device:TPU:25, one launch (start us, length us, event | category | flops | bytes accessed | tf_op | source)
XLA Modules:
  0.0 98.8 jit_solution(3869645223452623422)
XLA Ops:
  6.5 0.0 all-gather.2.cloned.1.call-start
  6.5 0.8 slice_reduce_fusion
  7.4 0.7 broadcast_compare_fusion
  8.0 1.2 %broadcast_select_fusion = (bf16[512,256]{1,0:T(8,128)(2,1)S(1)}, bf16[512,256]{1,0:T(8,128)(2,1)S(1)}, bf16[512,256]{1,0:T(8,128)(2,1)S(1)}) fusion(bf16[512,256]{1,0:T(8,128)(2,1)} %param.7, pred[512]{0:T(512)(128)(4,1)S(1)} %broadcast_compare_fusion, bf16[256]{0:T(256)(128)(2,1)S(1)} %get-tuple-element.13, bf16[512,256]{1,0:T(8,128)(2,1)} %param.9, ...), kind=kLoop, calls=%fused_computation.48 | loop fusion | flops 393216 | bytes 1574912 | tf_op jit(solution)/shard_map/jit(_where)/select_n | solution.py:47
  9.3 0.4 copy.27
  9.8 3.1 %collective-permute-start = (bf16[4,128,512]{2,0,1:T(4,128)(2,1)S(1)}, bf16[4,128,512]{2,0,1:T(4,128)(2,1)S(1)}, u32[]{:S(2)}, u32[]{:S(2)}) collective-permute-start(bf16[4,128,512]{2,0,1:T(4,128)(2,1)S(1)} %copy.27), channel_id=1, source_target_pairs={{0,4},{4,8},{8,12},{12,16},{16,20},{20,24},{24,28},{1,5},{5,9},{9,... | collective-permute-start | bytes 1572872 | tf_op jit(solution)/shard_map/ppermute | solution.py:15
  12.9 3.0 %collective-permute-start.1 = (bf16[4,128,512]{2,0,1:T(4,128)(2,1)S(1)}, bf16[4,128,512]{2,0,1:T(4,128)(2,1)}, u32[]{:S(2)}, u32[]{:S(2)}) collective-permute-start(bf16[4,128,512]{2,0,1:T(4,128)(2,1)S(1)} %copy.27), channel_id=1, source_target_pairs={{4,0},{8,4},{12,8},{16,12},{20,16},{24,20},{28,24},{5,1},{9,5},{13... | collective-permute-start | bytes 1572872 | tf_op jit(solution)/shard_map/ppermute | solution.py:15
  16.0 1.3 %collective-permute-start.2 = (bf16[4,128,512]{2,0,1:T(4,128)(2,1)S(1)}, bf16[4,128,512]{2,0,1:T(4,128)(2,1)}, u32[]{:S(2)}, u32[]{:S(2)}) collective-permute-start(bf16[4,128,512]{2,0,1:T(4,128)(2,1)S(1)} %copy.27), channel_id=1, source_target_pairs={{0,8},{4,12},{8,16},{12,20},{16,24},{20,28},{1,9},{5,13},{9,17},{1... | collective-permute-start | bytes 1572872 | tf_op jit(solution)/shard_map/ppermute | solution.py:15
  17.3 4.8 %collective-permute-start.3 = (bf16[4,128,512]{2,0,1:T(4,128)(2,1)S(1)}, bf16[4,128,512]{2,0,1:T(4,128)(2,1)}, u32[]{:S(2)}, u32[]{:S(2)}) collective-permute-start(bf16[4,128,512]{2,0,1:T(4,128)(2,1)S(1)} %copy.27), channel_id=1, source_target_pairs={{8,0},{12,4},{16,8},{20,12},{24,16},{28,20},{9,1},{13,5},{17,9},{2... | collective-permute-start | bytes 1572872 | tf_op jit(solution)/shard_map/ppermute | solution.py:15
  22.1 0.0 copy-done.2
  22.1 0.2 fusion.48
  22.3 0.1 fusion.36
  22.4 0.1 slice_compare_fusion
  22.4 0.3 copy.28
  22.8 0.3 copy.30
  23.1 0.2 reshape.65
  23.4 0.1 stack.38
  23.5 1.9 %collective-permute-done = bf16[4,128,512]{2,0,1:T(4,128)(2,1)S(1)} collective-permute-done((bf16[4,128,512]{2,0,1:T(4,128)(2,1)S(1)}, bf16[4,128,512]{2,0,1:T(4,128)(2,1)S(1)}, u32[]{:S(2)}, u32[]{:S(2)}) %collective-permute-start) | collective-permute-done | bytes 524320 | tf_op jit(solution)/shard_map/ppermute | solution.py:15
  25.4 0.3 slice.114
  25.7 12.1 %collective-permute-done.1 = bf16[4,128,512]{2,0,1:T(4,128)(2,1)} collective-permute-done((bf16[4,128,512]{2,0,1:T(4,128)(2,1)S(1)}, bf16[4,128,512]{2,0,1:T(4,128)(2,1)}, u32[]{:S(2)}, u32[]{:S(2)}) %collective-permute-start.1) | collective-permute-done | bytes 524320 | tf_op jit(solution)/shard_map/ppermute | solution.py:15
  37.7 1.2 %slice.119 = bf16[1,128,512]{2,0,1:T(2,128)(2,1)S(1)} slice(bf16[4,128,512]{2,0,1:T(4,128)(2,1)} %collective-permute-done.1), slice={[0:1], [0:128], [0:512]} | slice | bytes 262144 | tf_op jit(solution)/shard_map/slice | solution.py:73
  39.0 0.5 fusion.32
  39.5 0.4 copy_dynamic-update-slice_fusion
  40.0 0.6 fusion.33
  40.5 0.0 collective-permute-done.2
  40.6 1.6 %fusion.15 = bf16[4,7,128,512]{3,0,2,1:T(4,128)(2,1)S(1)} fusion(bf16[4,7,128,512]{3,0,2,1:T(4,128)(2,1)S(1)} %fusion.33, bf16[4,128,512]{2,0,1:T(4,128)(2,1)} %collective-permute-done.2, s32[4]{0:T(128)S(1)} %get-tuple-element.25), kind=kOutput, calls=%fused_computation.20 | convolution fusion | flops 2359312 | bytes 1049088 | tf_op jit(solution)/shard_map/lj,jkf->lkf/dot_general | solution.py:66
  42.2 0.6 fusion.17
  42.8 1.6 %fusion.19 = bf16[4,7,128,512]{3,0,2,1:T(4,128)(2,1)S(1)} fusion(bf16[4,7,128,512]{3,0,2,1:T(4,128)(2,1)S(1)} %fusion.17, bf16[4,128,512]{2,0,1:T(4,128)(2,1)} %collective-permute-done.1, s32[4]{0:T(128)S(1)} %get-tuple-element.26), kind=kOutput, calls=%fused_computation.24 | convolution fusion | flops 2359312 | bytes 1049088 | tf_op jit(solution)/shard_map/lj,jkf->lkf/dot_general | solution.py:66
  44.4 0.0 collective-permute-done.3
  44.4 1.6 %fusion.21 = bf16[4,7,128,512]{3,0,2,1:T(4,128)(2,1)S(1)} fusion(bf16[4,7,128,512]{3,0,2,1:T(4,128)(2,1)S(1)} %fusion.19, bf16[4,128,512]{2,0,1:T(4,128)(2,1)} %collective-permute-done.3, s32[4]{0:T(128)S(1)} %get-tuple-element.22), kind=kOutput, calls=%fused_computation.26 | convolution fusion | flops 2359312 | bytes 1049088 | tf_op jit(solution)/shard_map/lj,jkf->lkf/dot_general | solution.py:66
  46.1 2.9 %fusion.66 = (bf16[4,7,128,256]{3,0,2,1:T(4,128)(2,1)S(1)}, bf16[4,7,128,256]{3,0,2,1:T(4,128)(2,1)}) fusion(bf16[4,7,128,512]{3,0,2,1:T(4,128)(2,1)S(1)} %fusion.21), kind=kLoop, calls=%fused_computation.101 | loop fusion | bytes 7340032 | tf_op jit(solution)/shard_map/while/body/eval_jaxpr/slice | solution.py:24
  49.0 4.1 %copy.36 = bf16[4,7,128,256]{2,3,1,0:T(8,128)(2,1)} copy(bf16[4,7,128,256]{3,0,2,1:T(4,128)(2,1)} %get-tuple-element.28) | data formatting | bytes 3670016 | tf_op jit(solution)/shard_map/while/body/eval_jaxpr/slice | solution.py:23
  53.1 2.8 %copy.34 = bf16[4,7,128,256]{2,3,1,0:T(8,128)(2,1)} copy(bf16[4,7,128,256]{3,0,2,1:T(4,128)(2,1)S(1)} %get-tuple-element.27) | data formatting | bytes 3670016 | tf_op jit(solution)/shard_map/while/body/eval_jaxpr/slice | solution.py:24
  55.8 3.6 %fusion = (f32[4,4,128]{2,1,0:T(4,128)S(1)}, f32[4,4,128,7,128]{2,4,3,1,0:T(8,128)S(1)}) fusion(pred[4,7]{1,0:T(4,128)(4,1)S(1)} %stack.38, bf16[4,7,128,4,64]{2,4,3,1,0:T(8,128)(2,1)} %bitcast.83, bf16[4,128,4,64,1]{3,2,1,0,4:T(4,128)(2,1)S(1)} %bitcast.91), kind=kOutput, calls=%fused_computation.2 | convolution fusion | flops 240384000 | bytes 9445404 | tf_op jit(solution)/shard_map/while/body/eval_jaxpr/gqhd,gnkhd->ghqnk/dot_general | solution.py:27
  59.4 1.7 %fusion.1 = f32[4,4,128]{2,1,0:T(4,128)S(1)} fusion(f32[4,4,128,7,128]{2,4,3,1,0:T(8,128)S(1)} %get-tuple-element.39, f32[4,4,128]{2,1,0:T(4,128)S(1)} %get-tuple-element.38, pred[4,7]{1,0:T(4,128)(4,1)S(1)} %stack.38), kind=kLoop, calls=%fused_computation.3 | loop fusion | flops 7337984 | bytes 7356444 | tf_op jit(solution)/shard_map/while/body/eval_jaxpr/reduce_sum | solution.py:33
  61.1 0.0 copy-start.1
  61.1 2.0 %fusion.27 = bf16[4,128,4,64]{1,3,2,0:T(8,128)(2,1)S(1)} fusion(f32[4,4,128,7,128]{2,4,3,1,0:T(8,128)S(1)} %get-tuple-element.39, f32[4,4,128]{2,1,0:T(4,128)S(1)} %get-tuple-element.38, pred[4,7]{1,0:T(4,128)(4,1)S(1)} %stack.38, bf16[4,7,128,4,64]{2,4,3,1,0:T(8,128)(2,1)S(1)} %bitcast.92, f32[4,128,4]{1,2,0:T(4,128)S(1)} %bitcast.97), kind=kOutput, calls=%fused_computation.28 | convolution fusion | flops 242483200 | bytes 9453596 | tf_op jit(solution)/shard_map/while/body/eval_jaxpr/ghqnk,gnkhd->gqhd/dot_general | solution.py:35
  63.1 0.2 copy.41
  63.3 0.7 copy.73
  64.0 0.0 all-gather.2.cloned.1.call-update
  64.1 0.3 copy.42
  64.3 18.6 %all_to_all.16 = bf16[256,4,384]{0,2,1:T(8,128)(2,1)S(1)} all-to-all(bf16[256,4,384]{0,2,1:T(8,128)(2,1)S(1)} %bitcast.86), channel_id=1, replica_groups=mesh['seq'=8,'head'=4] {'head'}, dimensions={1} | all-to-all | bytes 1572864 | tf_op jit(solution)/shard_map/all_to_all | solution.py:91
  82.9 2.9 %all-gather.2.cloned.1.call-done = bf16[512,1024]{0,1:T(8,128)(2,1)} async-done(((bf16[512,256]{0,1:T(8,128)(2,1)}), bf16[512,1024]{0,1:T(8,128)(2,1)}) %all-gather.2.cloned.1.call-update) | async-done | bytes 1048592 | tf_op jit(solution)/shard_map/all_gather | solution.py:90
  85.8 1.3 %convolution_convert_fusion.7 = bf16[512,384]{1,0:T(8,128)(2,1)S(1)} fusion(bf16[512,1024]{0,1:T(8,128)(2,1)} %all-gather.2.cloned.1.call-done, bf16[4,256,384]{1,2,0:T(8,128)(2,1)S(1)} %bitcast.87), kind=kOutput, calls=%fused_computation.17 | convolution fusion | flops 100859904 | bytes 851968 | tf_op jit(solution)/shard_map/dot_general | solution.py:94
  87.1 1.3 %convolution_convert_fusion.6 = bf16[512,384]{1,0:T(8,128)(2,1)S(1)} fusion(bf16[512,1024]{0,1:T(8,128)(2,1)} %all-gather.2.cloned.1.call-done, bf16[4,256,384]{1,2,0:T(8,128)(2,1)S(1)} %bitcast.88), kind=kOutput, calls=%fused_computation.16 | convolution fusion | flops 100859904 | bytes 851968 | tf_op jit(solution)/shard_map/dot_general | solution.py:94
  88.4 1.3 %convolution_convert_fusion.5 = bf16[512,384]{1,0:T(8,128)(2,1)S(1)} fusion(bf16[512,1024]{0,1:T(8,128)(2,1)} %all-gather.2.cloned.1.call-done, bf16[4,256,384]{1,2,0:T(8,128)(2,1)S(1)} %bitcast.89), kind=kOutput, calls=%fused_computation.15 | convolution fusion | flops 100859904 | bytes 851968 | tf_op jit(solution)/shard_map/dot_general | solution.py:94
  89.7 1.3 %convolution_convert_fusion.4 = bf16[512,384]{1,0:T(8,128)(2,1)S(1)} fusion(bf16[512,1024]{0,1:T(8,128)(2,1)} %all-gather.2.cloned.1.call-done, bf16[4,256,384]{1,2,0:T(8,128)(2,1)S(1)} %bitcast.90), kind=kOutput, calls=%fused_computation.14 | convolution fusion | flops 100859904 | bytes 851968 | tf_op jit(solution)/shard_map/dot_general | solution.py:94
  91.0 0.9 add_convert_fusion
  (6 shorter events, 0.1 us)
Async XLA Ops:
  6.5 15.5 %copy-start.2 = (s32[4,4]{1,0:T(4,128)S(1)}, s32[4,4]{1,0:T(4,128)}, u32[]{:S(2)}) copy-start(s32[4,4]{1,0:T(4,128)} %param.12) | copy-start | bytes 196
  6.5 79.3 %all-gather.2.cloned.1.call-start = ((), (), s32[]{:S(2)}) async-start(), calls=%async_computation.1 | async-start | bytes 1310720 | tf_op jit(solution)/shard_map/all_gather | solution.py:90
  9.8 15.6 %collective-permute-start = (bf16[4,128,512]{2,0,1:T(4,128)(2,1)S(1)}, bf16[4,128,512]{2,0,1:T(4,128)(2,1)S(1)}, u32[]{:S(2)}, u32[]{:S(2)}) collective-permute-start(bf16[4,128,512]{2,0,1:T(4,128)(2,1)S(1)} %copy.27), channel_id=1, source_target_pairs={{0,4},{4,8},{8,12},{12,16},{16,20},{20,24},{24,28},{1,5},{5,9},{9,... | collective-permute-start | bytes 1572872 | tf_op jit(solution)/shard_map/ppermute | solution.py:15
  12.9 24.8 %collective-permute-start.1 = (bf16[4,128,512]{2,0,1:T(4,128)(2,1)S(1)}, bf16[4,128,512]{2,0,1:T(4,128)(2,1)}, u32[]{:S(2)}, u32[]{:S(2)}) collective-permute-start(bf16[4,128,512]{2,0,1:T(4,128)(2,1)S(1)} %copy.27), channel_id=1, source_target_pairs={{4,0},{8,4},{12,8},{16,12},{20,16},{24,20},{28,24},{5,1},{9,5},{13... | collective-permute-start | bytes 1572872 | tf_op jit(solution)/shard_map/ppermute | solution.py:15
  16.0 24.6 %collective-permute-start.2 = (bf16[4,128,512]{2,0,1:T(4,128)(2,1)S(1)}, bf16[4,128,512]{2,0,1:T(4,128)(2,1)}, u32[]{:S(2)}, u32[]{:S(2)}) collective-permute-start(bf16[4,128,512]{2,0,1:T(4,128)(2,1)S(1)} %copy.27), channel_id=1, source_target_pairs={{0,8},{4,12},{8,16},{12,20},{16,24},{20,28},{1,9},{5,13},{9,17},{1... | collective-permute-start | bytes 1572872 | tf_op jit(solution)/shard_map/ppermute | solution.py:15
  17.3 27.2 %collective-permute-start.3 = (bf16[4,128,512]{2,0,1:T(4,128)(2,1)S(1)}, bf16[4,128,512]{2,0,1:T(4,128)(2,1)}, u32[]{:S(2)}, u32[]{:S(2)}) collective-permute-start(bf16[4,128,512]{2,0,1:T(4,128)(2,1)S(1)} %copy.27), channel_id=1, source_target_pairs={{8,0},{12,4},{16,8},{20,12},{24,16},{28,20},{9,1},{13,5},{17,9},{2... | collective-permute-start | bytes 1572872 | tf_op jit(solution)/shard_map/ppermute | solution.py:15
  59.4 1.7 %copy-start = (bf16[4,7,128,256]{2,3,1,0:T(8,128)(2,1)S(1)}, bf16[4,7,128,256]{2,3,1,0:T(8,128)(2,1)}, u32[]{:S(2)}) copy-start(bf16[4,7,128,256]{2,3,1,0:T(8,128)(2,1)} %copy.34) | copy-start | bytes 5505028
  61.1 3.0 %copy-start.1 = (bf16[256,1536]{1,0:T(8,128)(2,1)S(1)}, bf16[256,1536]{1,0:T(8,128)(2,1)}, u32[]{:S(2)}) copy-start(bf16[256,1536]{1,0:T(8,128)(2,1)} %param.13) | copy-start | bytes 2359300
Sparse Core Ops, SparseCore 0:
  64.2 21.6 all-gather.1
where the time goes:
time: 99.5 us; the launch traced here: 98.8 us
  blocking collectives  18.6 us (19%)
  waiting for transfers between devices  16.9 us (17%)
  matrix products  16.2 us (16%)
  local copies, waits for them, and re-layouts  15.2 us (15%)
  between operations  13.6 us (14%)
  starting transfers between devices  12.3 us (12%)
  other arithmetic  6.07 us (6%)
    all_to_all x1, blocking collectives, on_device(): lax.all_to_all(w_out, 'head', split_axis=1, concat_axis=0, tiled=True)  18.6 us
    ppermute x4, waiting for transfers between devices, shifted(): return lax.ppermute(block, axis, route)  14 us
    ppermute x4, starting transfers between devices, shifted(): return lax.ppermute(block, axis, route)  12.3 us
    slice x2, local copies, waits for them, and re-layouts, attend_group(): value_grp = block_grp[..., feat_width:].reshape(shaped)  5.65 us
    dot_general x4, matrix products, on_device(): jnp.einsum('lj,jkf->lkf', picker, remote, preferred_element_type=jnp.floa...  5.49 us
    dot_general x4, matrix products, on_device(): jnp.dot(all_heads[:, member * feat_width:(member + 1) * feat_width], all_...  5.15 us
    slice x1, local copies, waits for them, and re-layouts, attend_group(): key_grp = block_grp[..., :feat_width].reshape(shaped)  4.12 us
    dot_general x1, matrix products, attend_group(): jnp.einsum('gqhd,gnkhd->ghqnk', query_grp, key_grp, preferred_element_typ...  3.57 us
  transfers between devices with their start and end apart: 5, of which 3 were waited for; matrix products, arithmetic and copies ran while one was open for 9% of the time, Pallas kernels for 0%

commit v1 on v0

v1 whole, which is shorter than its diff:
```python
import functools

import jax
import jax.numpy as jnp
from jax import lax
from jax.experimental import pallas as pl
from jax.experimental.pallas import tpu as pltpu
from jax.sharding import PartitionSpec as P

HD = 64
R = 2
CAP = 2
LANES = 128
MESH = pl.DeviceIdType.MESH
NEG = -1e30


def kernel(
    n_seq, n_head, bars_ref, masked_ref, mask_ref, q_ref, k_ref, v_ref, w_ref, out_ref,
    kv, qs, pack, got_a, got_b, got_c, got_d, rim, w_all, att, top, tot, acc,
    halo_send, halo_recv, rim_send, rim_recv, w_send, w_recv, w_own, att_send, att_recv,
):
    seq = lax.axis_index("seq")
    head = lax.axis_index("head")
    bar_count, bar_len, width = q_ref.shape
    tiles = width // LANES
    per_tile = LANES // HD
    out_cols = w_all.shape[2]
    columns = 2 * R
    got = (got_a, got_b, got_c, got_d)
    offsets = [c - R if c < R else c - R + 1 for c in range(columns)]
    low, high = R - 1, R

    def there(offset):
        return jnp.logical_and(seq + offset >= 0, seq + offset < n_seq)

    barrier = pltpu.get_barrier_semaphore()
    count = n_head - 1
    for offset in offsets:
        count = count + there(offset).astype(jnp.int32)

        @pl.when(there(offset))
        def _(offset=offset):
            pl.semaphore_signal(
                barrier, inc=1, device_id=(seq + offset, head), device_id_type=MESH
            )

    peers = [lax.rem(head + step, n_head) for step in range(1, n_head)]
    for peer in peers:
        pl.semaphore_signal(barrier, inc=1, device_id=(seq, peer), device_id_type=MESH)

    own_w = pltpu.make_async_copy(
        w_ref.at[:, pl.ds(pl.multiple_of(head * out_cols, LANES), out_cols)],
        w_all.at[head],
        w_own,
    )
    own_w.start()

    rows = lax.broadcasted_iota(jnp.int32, (bar_len, bar_len), 0)
    cols = lax.broadcasted_iota(jnp.int32, (bar_len, bar_len), 1)

    def flag(b):
        row = masked_ref[b : b + 1, :]
        return jnp.max(jnp.where(rows == cols, row, 0), axis=1, keepdims=True) == 1

    def replaced(value, row, hit):
        return jnp.where(hit, mask_ref[row : row + 1, :].astype(jnp.float32), value.astype(jnp.float32))

    for b in range(bar_count):
        hit = flag(b)
        kv[b, :, :width] = replaced(k_ref[b], 1, hit).astype(jnp.bfloat16)
        kv[b, :, width:] = replaced(v_ref[b], 2, hit).astype(jnp.bfloat16)

    listed = [[bars_ref[b, c] for c in range(columns)] for b in range(bar_count)]
    for c in (low, high, 0, columns - 1) if R == 2 else range(columns):
        before = jnp.int32(0)
        chosen = [jnp.int32(0)] * CAP
        for b in range(bar_count):
            used = (listed[b][c] >= 0).astype(jnp.int32)
            for slot in range(CAP):
                chosen[slot] = chosen[slot] + jnp.where(before == slot, used * b, 0)
            before = before + used
        for slot in range(CAP):
            pack[c, slot] = kv[chosen[slot]]

    pl.semaphore_wait(barrier, count)

    def halo(c):
        return pltpu.make_async_remote_copy(
            src_ref=pack.at[c],
            dst_ref=got[columns - 1 - c],
            send_sem=halo_send.at[c],
            recv_sem=halo_recv.at[columns - 1 - c],
            device_id=(seq + offsets[c], head),
            device_id_type=MESH,
        )

    def edge(side):
        return pltpu.make_async_remote_copy(
            src_ref=kv.at[bar_count - 1 if side else 0],
            dst_ref=rim.at[1 - side],
            send_sem=rim_send.at[side],
            recv_sem=rim_recv.at[1 - side],
            device_id=(seq + (1 if side else -1), head),
            device_id_type=MESH,
        )

    for c in [low, high] + [c for c in range(columns) if c not in (low, high)]:

        @pl.when(there(offsets[c]))
        def _(c=c):
            halo(c).start()
            if c in (low, high):
                edge(c - low).start()

        @pl.when(jnp.logical_not(there(offsets[c])))
        def _(c=c):
            got[c][...] = jnp.zeros(got[c].shape, got[c].dtype)
            if c in (low, high):
                rim[c - low] = jnp.zeros_like(rim[c - low])

    def w_copy(step):
        peer = peers[step]
        return pltpu.make_async_remote_copy(
            src_ref=w_ref.at[:, pl.ds(pl.multiple_of(peer * out_cols, LANES), out_cols)],
            dst_ref=w_all.at[head],
            send_sem=w_send.at[step],
            recv_sem=w_recv.at[step],
            device_id=(seq, peer),
            device_id_type=MESH,
        )

    for step in range(n_head - 1):
        w_copy(step).start()

    lane = lax.broadcasted_iota(jnp.int32, (bar_len, LANES), 1)
    scaling = HD ** -0.5
    for b in range(bar_count):
        query = replaced(q_ref[b], 0, flag(b)) * scaling
        for t in range(tiles):
            part = query[:, t * LANES : (t + 1) * LANES]
            for h in range(per_tile):
                qs[b, t, h * bar_len : (h + 1) * bar_len, :] = jnp.where(
                    lane // HD == h, part, 0.0
                ).astype(jnp.bfloat16)

    def update(b, t, blocks, first=False, last=False):
        k_at = slice(t * LANES, (t + 1) * LANES)
        v_at = slice(width + t * LANES, width + (t + 1) * LANES)
        query = qs[b, t]
        scores = []
        for ref, index, usable in blocks:
            s = lax.dot_general(
                query, ref[index + (slice(None), k_at)], (((1,), (1,)), ((), ())),
                preferred_element_type=jnp.float32,
            )
            if usable is not None:
                s = s + jnp.where(usable, 0.0, NEG).astype(jnp.float32)
            scores.append(s)
        wide = functools.reduce(jnp.maximum, scores)
        peak = jnp.max(wide, axis=1, keepdims=True)
        if not first:
            old = top[b, t][:, :1]
            peak = jnp.maximum(peak, old)
            fade = jnp.exp(old - peak)
        raised = [jnp.exp(s - peak) for s in scores]
        total = jnp.sum(functools.reduce(jnp.add, raised), axis=1, keepdims=True)
        rounded = jnp.concatenate([r.astype(jnp.bfloat16) for r in raised], axis=1)
        value = jnp.concatenate([ref[index + (slice(None), v_at)] for ref, index, _ in blocks], axis=0)
        weighted = jnp.dot(rounded, value, preferred_element_type=jnp.float32)
        if not first:
            total = total + tot[b, t][:, :1] * fade
            weighted = weighted + acc[b, t] * fade
        if not last:
            top[b, t] = jnp.broadcast_to(peak, top.shape[2:])
            tot[b, t] = jnp.broadcast_to(total, tot.shape[2:])
            acc[b, t] = weighted
            return None
        done = weighted / total
        result = done[:bar_len]
        for h in range(1, per_tile):
            result = jnp.where(lane // HD == h, done[h * bar_len : (h + 1) * bar_len], result)
        return result.astype(jnp.bfloat16)

    for b in range(bar_count):
        blocks = [(kv, (n,), None) for n in range(max(b - 1, 0), min(b + 2, bar_count))]
        for t in range(tiles):
            update(b, t, blocks, first=True)

    def listed_block(b, c):
        wanted = listed[b][c]
        slot = jnp.int32(0)
        for other in range(bar_count):
            held = listed[other][c]
            slot = slot + jnp.logical_and(held >= 0, held < wanted).astype(jnp.int32)
        return (got[c], (jnp.minimum(slot, CAP - 1),), wanted >= 0)

    far = [c for c in range(columns) if c not in (low, high)]
    for c in far:

        @pl.when(there(offsets[c]))
        def _(c=c):
            halo(columns - 1 - c).wait_recv()

    for b in range(bar_count):
        for t in range(tiles):
            update(b, t, [listed_block(b, c) for c in far])

    for c in (low, high):

        @pl.when(there(offsets[c]))
        def _(c=c):
            halo(columns - 1 - c).wait_recv()
            edge(high - c).wait_recv()

    twin = head + 1 - 2 * lax.rem(head, 2)
    across = lax.rem(head + 2, n_head)

    def att_copy(b, kind):
        slot = across if kind == 2 else head
        return pltpu.make_async_remote_copy(
            src_ref=att.at[slot, b],
            dst_ref=att.at[slot, b],
            send_sem=att_send.at[b, kind],
            recv_sem=att_recv.at[b, kind],
            device_id=(seq, across if kind == 1 else twin),
            device_id_type=MESH,
        )

    def relay(b):
        att_copy(b, 1).wait_recv()
        att_copy(b, 2).start()

    order = [0, bar_count - 1] + list(range(1, bar_count - 1))
    for place, b in enumerate(order):
        blocks = [listed_block(b, c) for c in (low, high)]
        if b == 0:
            blocks.append((rim, (0,), there(-1)))
        if b == bar_count - 1:
            blocks.append((rim, (1,), there(1)))
        for t in range(tiles):
            att[head, b, :, t * LANES : (t + 1) * LANES] = update(b, t, blocks, last=True)
        att_copy(b, 1).start()
        att_copy(b, 0).start()
        if place > 1:
            relay(order[place - 2])
    own_w.wait()
    for step in range(n_head - 1):
        w_copy(step).wait_recv()

    def project(b):
        att_copy(b, 0).wait_recv()
        att_copy(b, 2).wait_recv()
        summed = None
        for member in range(n_head):
            term = jnp.dot(att[member, b], w_all[member], preferred_element_type=jnp.float32)
            term = term.astype(jnp.bfloat16).astype(jnp.float32)
            summed = term if summed is None else summed + term
        out_ref[b] = summed.astype(jnp.bfloat16)

    for place, b in enumerate(order):
        if place >= len(order) - 2:
            pass
        elif place + 2 < len(order):
            relay(order[place + 2])
        project(b)

    for c in range(columns):

        @pl.when(there(offsets[c]))
        def _(c=c):
            halo(c).wait_send()
            if c in (low, high):
                edge(c - low).wait_send()

    for step in range(n_head - 1):
        w_copy(step).wait_send()
    for b in range(bar_count):
        for kind in range(3):
            att_copy(b, kind).wait_send()


def solution(mesh):
    n_seq, n_head = mesh.shape["seq"], mesh.shape["head"]

    def on_device(queries, keys, values, masked, mask_qkv, key_bars, w_out):
        tokens, width = queries.shape
        bars = key_bars.shape[0]
        length = tokens // bars
        cols = w_out.shape[1] // n_head
        tiles, rows = width // LANES, LANES // HD * length
        shaped = [x.reshape(bars, length, width) for x in (queries, keys, values)]
        vmem = pl.BlockSpec(memory_space=pltpu.VMEM)
        dma = pltpu.SemaphoreType.DMA
        out = pl.pallas_call(
            functools.partial(kernel, n_seq, n_head),
            out_shape=jax.ShapeDtypeStruct((bars, length, cols), jnp.bfloat16),
            in_specs=[pl.BlockSpec(memory_space=pltpu.SMEM)] + [vmem] * 6,
            out_specs=vmem,
            scratch_shapes=[
                pltpu.VMEM((bars, length, 2 * width), jnp.bfloat16),
                pltpu.VMEM((bars, tiles, rows, LANES), jnp.bfloat16),
                pltpu.VMEM((2 * R, CAP, length, 2 * width), jnp.bfloat16),
            ]
            + [pltpu.VMEM((CAP, length, 2 * width), jnp.bfloat16)] * (2 * R)
            + [
                pltpu.VMEM((2, length, 2 * width), jnp.bfloat16),
                pltpu.VMEM((n_head, width, cols), jnp.bfloat16),
                pltpu.VMEM((n_head, bars, length, width), jnp.bfloat16),
                pltpu.VMEM((bars, tiles, rows, LANES), jnp.float32),
                pltpu.VMEM((bars, tiles, rows, LANES), jnp.float32),
                pltpu.VMEM((bars, tiles, rows, LANES), jnp.float32),
                dma((2 * R,)),
                dma((2 * R,)),
                dma((2,)),
                dma((2,)),
                dma((n_head - 1,)),
                dma((n_head - 1,)),
                dma,
                dma((bars, 3)),
                dma((bars, 3)),
            ],
            compiler_params=pltpu.CompilerParams(
                collective_id=0, has_side_effects=True, vmem_limit_bytes=48 * 1024 * 1024
            ),
            name="bar_attention",
        )(key_bars, masked.reshape(bars, length), mask_qkv, *shaped, w_out)
        return out.reshape(tokens, cols)

    placed = (
        P("seq", "head"),
        P("seq", "head"),
        P("seq", "head"),
        P("seq"),
        P(None, "head"),
        P("seq", None),
        P("head", None),
    )
    return jax.shard_map(
        on_device, mesh=mesh, in_specs=placed, out_specs=P("seq", "head"), check_vma=False
    )
```

time: 99.5 us -> 39.7 us (0.40)
  the two profiles are of different devices: /device:TPU:25 before, /device:TPU:1 now
where the time goes in v1:
time: 39.7 us; the launch traced here: 39.4 us
  Pallas kernels  33.9 us (85%)
  local copies, waits for them, and re-layouts  5.44 us (14%)
    pallas_call x1, Pallas kernels, on_device(): pl.pallas_call(functools.partial(kernel, n_seq, n_head), out_shape=jax.Sh...  33.9 us
    unnamed x15, local copies, waits for them, and re-layouts  5.44 us

profile of v1, /device:TPU:1, one launch (start us, length us, event | category | flops | bytes accessed | tf_op | source)
XLA Modules:
  0.0 39.4 jit_solution(14747254598923597816)
XLA Ops:
  0.0 0.0 copy-start.6
  0.0 0.0 copy-start.5
  0.0 0.0 copy-start.4
  0.0 0.7 %copy-done.6 = bf16[3,256]{1,0:T(4,128)(2,1)S(1)} copy-done((bf16[3,256]{1,0:T(4,128)(2,1)S(1)}, bf16[3,256]{1,0:T(4,128)(2,1)}, u32[]{:S(2)}) %copy-start.6) | copy-done | bytes 1560
  0.7 0.0 copy-done.5
  0.7 0.0 copy-done.4
  0.7 0.0 copy-start
  0.7 1.1 %copy-done = bf16[256,1536]{1,0:T(8,128)(2,1)S(1)} copy-done((bf16[256,1536]{1,0:T(8,128)(2,1)S(1)}, bf16[256,1536]{1,0:T(8,128)(2,1)}, u32[]{:S(2)}) %copy-start) | copy-done | bytes 786456
  1.8 0.0 copy-start.1
  1.9 0.9 %copy-done.1 = bf16[512,256]{1,0:T(8,128)(2,1)S(1)} copy-done((bf16[512,256]{1,0:T(8,128)(2,1)S(1)}, bf16[512,256]{1,0:T(8,128)(2,1)}, u32[]{:S(2)}) %copy-start.1) | copy-done | bytes 262168
  2.8 0.0 copy-start.2
  2.8 0.9 %copy-done.2 = bf16[512,256]{1,0:T(8,128)(2,1)S(1)} copy-done((bf16[512,256]{1,0:T(8,128)(2,1)S(1)}, bf16[512,256]{1,0:T(8,128)(2,1)}, u32[]{:S(2)}) %copy-start.2) | copy-done | bytes 262168
  3.7 0.0 copy-start.3
  3.8 0.9 %copy-done.3 = bf16[512,256]{1,0:T(8,128)(2,1)S(1)} copy-done((bf16[512,256]{1,0:T(8,128)(2,1)S(1)}, bf16[512,256]{1,0:T(8,128)(2,1)}, u32[]{:S(2)}) %copy-start.3) | copy-done | bytes 262168
  4.7 33.9 %bar_attention.1 = bf16[4,128,384]{2,1,0:T(8,128)(2,1)S(1)} custom-call(s32[4,4]{1,0:T(4,128)S(1)} %copy-done.4, s32[4,128]{1,0:T(4,128)S(1)} %bitcast.9, bf16[3,256]{1,0:T(4,128)(2,1)S(1)} %copy-done.6, bf16[4,128,256]{2,1,0:T(8,128)(2,1)S(1)} %bitcast.6, bf16[4,128,256]{2,1,0:T(8,128)(2,1)S(1)} %bitcast.7, bf16[4,128,256]{2,1,0:T(8,128)(2,1)S(1)} %bitcast.8, ...), custom_call_target="tpu_custom_call" | custom-call | tf_op jit(solution)/shard_map/bar_attention/pallas_call | solution.py:295
  38.6 0.7 %copy.9 = bf16[512,384]{1,0:T(8,128)(2,1)} copy(bf16[512,384]{1,0:T(8,128)(2,1)S(1)} %bitcast.5) | data formatting | bytes 786432
Async XLA Ops:
  0.0 0.7 %copy-start.6 = (bf16[3,256]{1,0:T(4,128)(2,1)S(1)}, bf16[3,256]{1,0:T(4,128)(2,1)}, u32[]{:S(2)}) copy-start(bf16[3,256]{1,0:T(4,128)(2,1)} %mask_ref.1) | copy-start | bytes 4612
  0.0 0.7 %copy-start.5 = (s32[512]{0:T(512)S(1)}, s32[512]{0:T(512)}, u32[]{:S(2)}) copy-start(s32[512]{0:T(512)} %param.10) | copy-start | bytes 6148
  0.0 0.7 %copy-start.4 = (s32[4,4]{1,0:T(4,128)S(1)}, s32[4,4]{1,0:T(4,128)}, u32[]{:S(2)}) copy-start(s32[4,4]{1,0:T(4,128)} %bars_ref.1) | copy-start | bytes 196
  0.7 1.1 %copy-start = (bf16[256,1536]{1,0:T(8,128)(2,1)S(1)}, bf16[256,1536]{1,0:T(8,128)(2,1)}, u32[]{:S(2)}) copy-start(bf16[256,1536]{1,0:T(8,128)(2,1)} %w_ref.1) | copy-start | bytes 2359300
  1.8 0.9 %copy-start.1 = (bf16[512,256]{1,0:T(8,128)(2,1)S(1)}, bf16[512,256]{1,0:T(8,128)(2,1)}, u32[]{:S(2)}) copy-start(bf16[512,256]{1,0:T(8,128)(2,1)} %param.7) | copy-start | bytes 786436
  2.8 0.9 %copy-start.2 = (bf16[512,256]{1,0:T(8,128)(2,1)S(1)}, bf16[512,256]{1,0:T(8,128)(2,1)}, u32[]{:S(2)}) copy-start(bf16[512,256]{1,0:T(8,128)(2,1)} %param.8) | copy-start | bytes 786436
  3.7 0.9 %copy-start.3 = (bf16[512,256]{1,0:T(8,128)(2,1)S(1)}, bf16[512,256]{1,0:T(8,128)(2,1)}, u32[]{:S(2)}) copy-start(bf16[512,256]{1,0:T(8,128)(2,1)} %param.9) | copy-start | bytes 786436

commit v2 on v1

v2 whole, which is shorter than its diff:
```python
import functools

import jax
import jax.numpy as jnp
from jax import lax
from jax.experimental import pallas as pl
from jax.experimental.pallas import tpu as pltpu
from jax.sharding import PartitionSpec as P

HD = 64
R = 2
CAP = 2
CHUNK = 2
LANES = 128
MESH = pl.DeviceIdType.MESH
NEG = -1e30


def kernel(
    n_seq, n_head, bars_ref, masked_ref, mask_ref, q_hbm, k_hbm, v_hbm, w_ref, out_ref,
    q_ref, k_ref, v_ref, in_sem,    kv, qs, pack, got_refs, rim, w_all, att, top, tot, acc,
    halo_send, halo_recv, rim_send, rim_recv, w_send, w_recv, w_own, att_send, att_recv,
):
    seq = lax.axis_index("seq")
    head = lax.axis_index("head")
    bar_count, bar_len, width = q_ref.shape
    tiles = width // LANES
    per_tile = LANES // HD
    out_cols = w_all.shape[2]
    columns = 2 * R
    got = [got_refs[c * tiles : (c + 1) * tiles] for c in range(columns)]
    offsets = [c - R if c < R else c - R + 1 for c in range(columns)]
    low, high = R - 1, R

    def there(offset):
        return jnp.logical_and(seq + offset >= 0, seq + offset < n_seq)

    barrier = pltpu.get_barrier_semaphore()
    count = n_head - 1
    for offset in offsets:
        count = count + there(offset).astype(jnp.int32)

        @pl.when(there(offset))
        def _(offset=offset):
            pl.semaphore_signal(
                barrier, inc=1, device_id=(seq + offset, head), device_id_type=MESH
            )

    peers = [lax.rem(head + step, n_head) for step in range(1, n_head)]
    for peer in peers:
        pl.semaphore_signal(barrier, inc=1, device_id=(seq, peer), device_id_type=MESH)

    loads = [
        pltpu.make_async_copy(source, target, in_sem.at[n])
        for n, (source, target) in enumerate(((k_hbm, k_ref), (v_hbm, v_ref), (q_hbm, q_ref)))
    ]
    for load in loads:
        load.start()
    own_w = pltpu.make_async_copy(
        w_ref.at[:, pl.ds(pl.multiple_of(head * out_cols, LANES), out_cols)],
        w_all.at[head],
        w_own,
    )
    own_w.start()

    rows = lax.broadcasted_iota(jnp.int32, (bar_len, bar_len), 0)
    cols = lax.broadcasted_iota(jnp.int32, (bar_len, bar_len), 1)

    def flag(b):
        row = masked_ref[b : b + 1, :]
        return jnp.max(jnp.where(rows == cols, row, 0), axis=1, keepdims=True) == 1

    def replaced(value, row, hit):
        return jnp.where(hit, mask_ref[row : row + 1, :].astype(jnp.float32), value.astype(jnp.float32))

    loads[0].wait()
    loads[1].wait()
    for b in range(bar_count):
        hit = flag(b)
        key_eff = replaced(k_ref[b], 1, hit).astype(jnp.bfloat16)
        value_eff = replaced(v_ref[b], 2, hit).astype(jnp.bfloat16)
        for t in range(tiles):
            kv[t, b, :, :LANES] = key_eff[:, t * LANES : (t + 1) * LANES]
            kv[t, b, :, LANES:] = value_eff[:, t * LANES : (t + 1) * LANES]

    listed = [[bars_ref[b, c] for c in range(columns)] for b in range(bar_count)]
    for c in (low, high, 0, columns - 1) if R == 2 else range(columns):
        before = jnp.int32(0)
        chosen = [jnp.int32(0)] * CAP
        for b in range(bar_count):
            used = (listed[b][c] >= 0).astype(jnp.int32)
            for slot in range(CAP):
                chosen[slot] = chosen[slot] + jnp.where(before == slot, used * b, 0)
            before = before + used
        for slot in range(CAP):
            for t in range(tiles):
                pack[c, t, slot] = kv[t, chosen[slot]]

    pl.semaphore_wait(barrier, count)

    def halo(c, t):
        return pltpu.make_async_remote_copy(
            src_ref=pack.at[c, t],
            dst_ref=got[columns - 1 - c][t],
            send_sem=halo_send.at[c, t],
            recv_sem=halo_recv.at[columns - 1 - c, t],
            device_id=(seq + offsets[c], head),
            device_id_type=MESH,
        )

    def edge(side, t):
        return pltpu.make_async_remote_copy(
            src_ref=kv.at[t, bar_count - 1 if side else 0],
            dst_ref=rim.at[1 - side, t],
            send_sem=rim_send.at[side, t],
            recv_sem=rim_recv.at[1 - side, t],
            device_id=(seq + (1 if side else -1), head),
            device_id_type=MESH,
        )

    far = [c for c in range(columns) if c not in (low, high)]
    for t in range(tiles):
        for c in [low, high] + far:

            @pl.when(there(offsets[c]))
            def _(c=c, t=t):
                if c in (low, high):
                    edge(c - low, t).start()
                halo(c, t).start()

            @pl.when(jnp.logical_not(there(offsets[c])))
            def _(c=c, t=t):
                got[c][t][...] = jnp.zeros(got[c][t].shape, got[c][t].dtype)
                if c in (low, high):
                    rim[c - low, t] = jnp.zeros(rim.shape[2:], rim.dtype)

    def w_copy(step):
        peer = peers[step]
        return pltpu.make_async_remote_copy(
            src_ref=w_ref.at[:, pl.ds(pl.multiple_of(peer * out_cols, LANES), out_cols)],
            dst_ref=w_all.at[head],
            send_sem=w_send.at[step],
            recv_sem=w_recv.at[step],
            device_id=(seq, peer),
            device_id_type=MESH,
        )

    for step in range(n_head - 1):
        w_copy(step).start()

    lane = lax.broadcasted_iota(jnp.int32, (bar_len, LANES), 1)
    scaling = HD ** -0.5
    loads[2].wait()
    for b in range(bar_count):
        query = replaced(q_ref[b], 0, flag(b)) * scaling
        for t in range(tiles):
            part = query[:, t * LANES : (t + 1) * LANES]
            for h in range(per_tile):
                qs[b, t, h * bar_len : (h + 1) * bar_len, :] = jnp.where(
                    lane // HD == h, part, 0.0
                ).astype(jnp.bfloat16)

    def update(b, t, blocks, first=False, last=False):
        k_at, v_at = slice(0, LANES), slice(LANES, 2 * LANES)
        query = qs[b, t]
        scores = []
        for ref, index, usable in blocks:
            s = lax.dot_general(
                query, ref[index + (slice(None), k_at)], (((1,), (1,)), ((), ())),
                preferred_element_type=jnp.float32,
            )
            if usable is not None:
                s = s + jnp.where(usable, 0.0, NEG).astype(jnp.float32)
            scores.append(s)
        wide = functools.reduce(jnp.maximum, scores)
        peak = jnp.max(wide, axis=1, keepdims=True)
        if not first:
            old = top[b, t][:, :1]
            peak = jnp.maximum(peak, old)
            fade = jnp.exp(old - peak)
        raised = [jnp.exp(s - peak) for s in scores]
        total = jnp.sum(functools.reduce(jnp.add, raised), axis=1, keepdims=True)
        rounded = jnp.concatenate([r.astype(jnp.bfloat16) for r in raised], axis=1)
        value = jnp.concatenate([ref[index + (slice(None), v_at)] for ref, index, _ in blocks], axis=0)
        weighted = jnp.dot(rounded, value, preferred_element_type=jnp.float32)
        if not first:
            total = total + tot[b, t][:, :1] * fade
            weighted = weighted + acc[b, t] * fade
        if not last:
            top[b, t] = jnp.broadcast_to(peak, top.shape[2:])
            tot[b, t] = jnp.broadcast_to(total, tot.shape[2:])
            acc[b, t] = weighted
            return None
        done = weighted / total
        result = done[:bar_len]
        for h in range(1, per_tile):
            result = jnp.where(lane // HD == h, done[h * bar_len : (h + 1) * bar_len], result)
        return result.astype(jnp.bfloat16)

    for t in range(tiles):
        for b in range(bar_count):
            blocks = [(kv, (t, n), None) for n in range(max(b - 1, 0), min(b + 2, bar_count))]
            update(b, t, blocks, first=True)

    def listed_block(b, c, t):
        wanted = listed[b][c]
        slot = jnp.int32(0)
        for other in range(bar_count):
            held = listed[other][c]
            slot = slot + jnp.logical_and(held >= 0, held < wanted).astype(jnp.int32)
        return (got[c][t], (jnp.minimum(slot, CAP - 1),), wanted >= 0)

    twin = head + 1 - 2 * lax.rem(head, 2)
    across = lax.rem(head + 2, n_head)
    chunks = bar_count // CHUNK

    def att_copy(t, g, kind):
        slot = across if kind == 2 else head
        part = att.at[slot, t, g * CHUNK : (g + 1) * CHUNK]
        return pltpu.make_async_remote_copy(
            src_ref=part,
            dst_ref=part,
            send_sem=att_send.at[t, g, kind],
            recv_sem=att_recv.at[t, g, kind],
            device_id=(seq, across if kind == 1 else twin),
            device_id_type=MESH,
        )

    def relay(t, g):
        att_copy(t, g, 1).wait_recv()
        att_copy(t, g, 2).start()

    for t in range(tiles):
        for c in far:

            @pl.when(there(offsets[c]))
            def _(c=c, t=t):
                halo(columns - 1 - c, t).wait_recv()

        for b in range(bar_count):
            update(b, t, [listed_block(b, c, t) for c in far])
        if t > 0:
            for g in range(chunks):
                relay(t - 1, g)
        for c in (low, high):

            @pl.when(there(offsets[c]))
            def _(c=c, t=t):
                halo(columns - 1 - c, t).wait_recv()
                edge(high - c, t).wait_recv()

        for g in range(chunks):
            for b in range(g * CHUNK, (g + 1) * CHUNK):
                blocks = [listed_block(b, c, t) for c in (low, high)]
                if b == 0:
                    blocks.append((rim, (0, t), there(-1)))
                if b == bar_count - 1:
                    blocks.append((rim, (1, t), there(1)))
                att[head, t, b] = update(b, t, blocks, last=True)
            att_copy(t, g, 1).start()
            att_copy(t, g, 0).start()

    own_w.wait()
    for step in range(n_head - 1):
        w_copy(step).wait_recv()
    for g in range(chunks):
        relay(tiles - 1, g)
    for g in range(chunks):
        for t in range(tiles):
            att_copy(t, g, 0).wait_recv()
            att_copy(t, g, 2).wait_recv()
        for b in range(g * CHUNK, (g + 1) * CHUNK):
            summed = None
            for member in range(n_head):
                lhs = jnp.concatenate([att[member, t, b] for t in range(tiles)], axis=1)
                term = jnp.dot(lhs, w_all[member], preferred_element_type=jnp.float32)
                term = term.astype(jnp.bfloat16).astype(jnp.float32)
                summed = term if summed is None else summed + term
            out_ref[b] = summed.astype(jnp.bfloat16)

    for t in range(tiles):
        for c in range(columns):

            @pl.when(there(offsets[c]))
            def _(c=c, t=t):
                halo(c, t).wait_send()
                if c in (low, high):
                    edge(c - low, t).wait_send()

        for g in range(chunks):
            for kind in range(3):
                att_copy(t, g, kind).wait_send()
    for step in range(n_head - 1):
        w_copy(step).wait_send()


def solution(mesh):
    n_seq, n_head = mesh.shape["seq"], mesh.shape["head"]

    def on_device(queries, keys, values, masked, mask_qkv, key_bars, w_out):
        tokens, width = queries.shape
        bars = key_bars.shape[0]
        length = tokens // bars
        cols = w_out.shape[1] // n_head
        tiles, rows = width // LANES, LANES // HD * length
        shaped = [x.reshape(bars, length, width) for x in (queries, keys, values)]
        vmem = pl.BlockSpec(memory_space=pltpu.VMEM)
        dma = pltpu.SemaphoreType.DMA
        out = pl.pallas_call(
            functools.partial(kernel, n_seq, n_head),
            out_shape=jax.ShapeDtypeStruct((bars, length, cols), jnp.bfloat16),
            in_specs=[pl.BlockSpec(memory_space=pltpu.SMEM)] + [vmem] * 2 + [pl.BlockSpec(memory_space=pl.ANY)] * 4,
            out_specs=vmem,
            scratch_shapes=[pltpu.VMEM((bars, length, width), jnp.bfloat16)] * 3
            + [
                dma((3,)),
                pltpu.VMEM((tiles, bars, length, 2 * LANES), jnp.bfloat16),
                pltpu.VMEM((bars, tiles, rows, LANES), jnp.bfloat16),
                pltpu.VMEM((2 * R, tiles, CAP, length, 2 * LANES), jnp.bfloat16),
                [pltpu.VMEM((CAP, length, 2 * LANES), jnp.bfloat16)] * (2 * R * tiles),
                pltpu.VMEM((2, tiles, length, 2 * LANES), jnp.bfloat16),
                pltpu.VMEM((n_head, width, cols), jnp.bfloat16),
                pltpu.VMEM((n_head, tiles, bars, length, LANES), jnp.bfloat16),
                pltpu.VMEM((bars, tiles, rows, LANES), jnp.float32),
                pltpu.VMEM((bars, tiles, rows, LANES), jnp.float32),
                pltpu.VMEM((bars, tiles, rows, LANES), jnp.float32),
                dma((2 * R, tiles)),
                dma((2 * R, tiles)),
                dma((2, tiles)),
                dma((2, tiles)),
                dma((n_head - 1,)),
                dma((n_head - 1,)),
                dma,
                dma((tiles, bars // CHUNK, 3)),
                dma((tiles, bars // CHUNK, 3)),
            ],
            compiler_params=pltpu.CompilerParams(
                collective_id=0, has_side_effects=True
            ),
            name="bar_attention",
        )(key_bars, masked.reshape(bars, length), mask_qkv, *shaped, w_out)
        return out.reshape(tokens, cols)

    placed = (
        P("seq", "head"),
        P("seq", "head"),
        P("seq", "head"),
        P("seq"),
        P(None, "head"),
        P("seq", None),
        P("head", None),
    )
    return jax.shard_map(
        on_device, mesh=mesh, in_specs=placed, out_specs=P("seq", "head"), check_vma=False
    )
```

time: 39.7 us -> 33.7 us (0.85)
  the two profiles are of different devices: /device:TPU:1 before, /device:TPU:25 now
where the time goes in v2:
time: 33.7 us; the launch traced here: 33.5 us
  Pallas kernels  31.7 us (94%)
  local copies, waits for them, and re-layouts  1.78 us (5%)
    pallas_call x1, Pallas kernels, on_device(): pl.pallas_call(functools.partial(kernel, n_seq, n_head), out_shape=jax.Sh...  31.7 us
    unnamed x1, local copies, waits for them, and re-layouts  1.78 us

profile of v2, /device:TPU:25, one launch (start us, length us, event | category | flops | bytes accessed | tf_op | source)
XLA Modules:
  0.0 33.5 jit_solution(6097322245255623071)
XLA Ops:
  0.0 31.7 %bar_attention.1 = bf16[4,128,384]{2,1,0:T(8,128)(2,1)} custom-call(s32[4,4]{1,0:T(4,128)} %bars_ref.1, s32[4,128]{1,0:T(4,128)} %bitcast.9, bf16[3,256]{1,0:T(4,128)(2,1)} %mask_ref.1, bf16[4,128,256]{2,1,0:T(8,128)(2,1)} %bitcast.6, bf16[4,128,256]{2,1,0:T(8,128)(2,1)} %bitcast.7, bf16[4,128,256]{2,1,0:T(8,128)(2,1)} %bitcast.8, bf16[256,1536]{1,0:T(8,128)(2,1)} %w_ref.1), custom_call_target="tpu_custom_call" | custom-call | tf_op jit(solution)/shard_map/bar_attention/pallas_call | solution.py:309
  31.7 1.8 %copy.9 = bf16[512,384]{1,0:T(8,128)(2,1)} copy(bf16[512,384]{1,0:T(8,128)(2,1)} %bitcast.5) | data formatting | bytes 786432

commit v3 on v2

--- a/solution.py
+++ b/solution.py
@@ -10,7 +10,7 @@
 HD = 64
 R = 2
 CAP = 2
-CHUNK = 2
+CHUNK = 1
 LANES = 128
 MESH = pl.DeviceIdType.MESH
 NEG = -1e30
@@ -50,12 +50,16 @@
     for peer in peers:
         pl.semaphore_signal(barrier, inc=1, device_id=(seq, peer), device_id_type=MESH)
 
-    loads = [
-        pltpu.make_async_copy(source, target, in_sem.at[n])
-        for n, (source, target) in enumerate(((k_hbm, k_ref), (v_hbm, v_ref), (q_hbm, q_ref)))
-    ]
-    for load in loads:
-        load.start()
+    bar_order = [bar_count - 1, 0] + list(range(1, bar_count - 1))
+    loads = {}
+    for n, (source, target) in enumerate(((k_hbm, k_ref), (v_hbm, v_ref))):
+        for b in range(bar_count):
+            loads[n, b] = pltpu.make_async_copy(source.at[b], target.at[b], in_sem.at[n, b])
+    for b in bar_order:
+        loads[0, b].start()
+        loads[1, b].start()
+    q_load = pltpu.make_async_copy(q_hbm, q_ref, in_sem.at[2, 0])
+    q_load.start()
     own_w = pltpu.make_async_copy(
         w_ref.at[:, pl.ds(pl.multiple_of(head * out_cols, LANES), out_cols)],
         w_all.at[head],
@@ -73,9 +77,9 @@
     def replaced(value, row, hit):
         return jnp.where(hit, mask_ref[row : row + 1, :].astype(jnp.float32), value.astype(jnp.float32))
 
-    loads[0].wait()
-    loads[1].wait()
-    for b in range(bar_count):
+    def prepare(b):
+        loads[0, b].wait()
+        loads[1, b].wait()
         hit = flag(b)
         key_eff = replaced(k_ref[b], 1, hit).astype(jnp.bfloat16)
         value_eff = replaced(v_ref[b], 2, hit).astype(jnp.bfloat16)
@@ -83,8 +87,12 @@
             kv[t, b, :, :LANES] = key_eff[:, t * LANES : (t + 1) * LANES]
             kv[t, b, :, LANES:] = value_eff[:, t * LANES : (t + 1) * LANES]
 
+    for b in bar_order[:2]:
+        prepare(b)
+
     listed = [[bars_ref[b, c] for c in range(columns)] for b in range(bar_count)]
-    for c in (low, high, 0, columns - 1) if R == 2 else range(columns):
+    picks = []
+    for c in range(columns):
         before = jnp.int32(0)
         chosen = [jnp.int32(0)] * CAP
         for b in range(bar_count):
@@ -92,9 +100,7 @@
             for slot in range(CAP):
                 chosen[slot] = chosen[slot] + jnp.where(before == slot, used * b, 0)
             before = before + used
-        for slot in range(CAP):
-            for t in range(tiles):
-                pack[c, t, slot] = kv[t, chosen[slot]]
+        picks.append(chosen)
 
     pl.semaphore_wait(barrier, count)
 
@@ -119,12 +125,22 @@
         )
 
     far = [c for c in range(columns) if c not in (low, high)]
+    for c in (low, high):
+
+        @pl.when(there(offsets[c]))
+        def _(c=c):
+            edge(c - low, 0).start()
+
+    for b in bar_order[2:]:
+        prepare(b)
     for t in range(tiles):
-        for c in [low, high] + far:
+        for c in far + [low, high]:
+            for slot in range(CAP):
+                pack[c, t, slot] = kv[t, picks[c][slot]]
 
             @pl.when(there(offsets[c]))
             def _(c=c, t=t):
-                if c in (low, high):
+                if c in (low, high) and t > 0:
                     edge(c - low, t).start()
                 halo(c, t).start()
 
@@ -150,7 +166,7 @@
 
     lane = lax.broadcasted_iota(jnp.int32, (bar_len, LANES), 1)
     scaling = HD ** -0.5
-    loads[2].wait()
+    q_load.wait()
     for b in range(bar_count):
         query = replaced(q_ref[b], 0, flag(b)) * scaling
         for t in range(tiles):
@@ -313,7 +329,7 @@
             out_specs=vmem,
             scratch_shapes=[pltpu.VMEM((bars, length, width), jnp.bfloat16)] * 3
             + [
-                dma((3,)),
+                dma((3, bars)),
                 pltpu.VMEM((tiles, bars, length, 2 * LANES), jnp.bfloat16),
                 pltpu.VMEM((bars, tiles, rows, LANES), jnp.bfloat16),
                 pltpu.VMEM((2 * R, tiles, CAP, length, 2 * LANES), jnp.bfloat16),

time: 33.7 us -> 32.1 us (0.953)
  Pallas kernels: 31.7 us -> 30.1 us
    pallas_call x1, Pallas kernels: 31.7 us -> 30.1 us  [on_device(): pl.pallas_call(functools.partial(kernel, n_seq, n_head), out_shape=jax.Sh...]
where the time goes in v3:
time: 32.1 us; the launch traced here: 31.9 us
  Pallas kernels  30.1 us (94%)
  local copies, waits for them, and re-layouts  1.78 us (6%)
    pallas_call x1, Pallas kernels, on_device(): pl.pallas_call(functools.partial(kernel, n_seq, n_head), out_shape=jax.Sh...  30.1 us
    unnamed x1, local copies, waits for them, and re-layouts  1.78 us

profile of v3, /device:TPU:25, one launch (start us, length us, event | category | flops | bytes accessed | tf_op | source)
XLA Modules:
  0.0 31.9 jit_solution(17764998386419016779)
XLA Ops:
  0.0 30.1 %bar_attention.1 = bf16[4,128,384]{2,1,0:T(8,128)(2,1)} custom-call(s32[4,4]{1,0:T(4,128)} %bars_ref.1, s32[4,128]{1,0:T(4,128)} %bitcast.9, bf16[3,256]{1,0:T(4,128)(2,1)} %mask_ref.1, bf16[4,128,256]{2,1,0:T(8,128)(2,1)} %bitcast.6, bf16[4,128,256]{2,1,0:T(8,128)(2,1)} %bitcast.7, bf16[4,128,256]{2,1,0:T(8,128)(2,1)} %bitcast.8, bf16[256,1536]{1,0:T(8,128)(2,1)} %w_ref.1), custom_call_target="tpu_custom_call" | custom-call | tf_op jit(solution)/shard_map/bar_attention/pallas_call | solution.py:325
  30.1 1.8 %copy.9 = bf16[512,384]{1,0:T(8,128)(2,1)} copy(bf16[512,384]{1,0:T(8,128)(2,1)} %bitcast.5) | data formatting | bytes 786432

commit v4 on v3

--- a/solution.py
+++ b/solution.py
@@ -17,8 +17,8 @@
 
 
 def kernel(
-    n_seq, n_head, bars_ref, masked_ref, mask_ref, q_hbm, k_hbm, v_hbm, w_ref, out_ref,
-    q_ref, k_ref, v_ref, in_sem,    kv, qs, pack, got_refs, rim, w_all, att, top, tot, acc,
+    n_seq, n_head, bars_hbm, masked_hbm, mask_hbm, q_hbm, k_hbm, v_hbm, w_ref, out_ref,
+    bars_ref, masked_ref, mask_ref, small_sem, q_ref, k_ref, v_ref, in_sem,    kv, qs, pack, got_refs, rim, w_all, att, top, tot, acc,
     halo_send, halo_recv, rim_send, rim_recv, w_send, w_recv, w_own, att_send, att_recv,
 ):
     seq = lax.axis_index("seq")
@@ -50,6 +50,14 @@
     for peer in peers:
         pl.semaphore_signal(barrier, inc=1, device_id=(seq, peer), device_id_type=MESH)
 
+    small = [
+        pltpu.make_async_copy(source, target, small_sem.at[n])
+        for n, (source, target) in enumerate(
+            ((masked_hbm, masked_ref), (mask_hbm, mask_ref), (bars_hbm, bars_ref))
+        )
+    ]
+    for load in small:
+        load.start()
     bar_order = [bar_count - 1, 0] + list(range(1, bar_count - 1))
     loads = {}
     for n, (source, target) in enumerate(((k_hbm, k_ref), (v_hbm, v_ref))):
@@ -87,6 +95,8 @@
             kv[t, b, :, :LANES] = key_eff[:, t * LANES : (t + 1) * LANES]
             kv[t, b, :, LANES:] = value_eff[:, t * LANES : (t + 1) * LANES]
 
+    for load in small:
+        load.wait()
     for b in bar_order[:2]:
         prepare(b)
 
@@ -133,22 +143,22 @@
 
     for b in bar_order[2:]:
         prepare(b)
-    for t in range(tiles):
-        for c in far + [low, high]:
-            for slot in range(CAP):
-                pack[c, t, slot] = kv[t, picks[c][slot]]
-
-            @pl.when(there(offsets[c]))
-            def _(c=c, t=t):
-                if c in (low, high) and t > 0:
-                    edge(c - low, t).start()
-                halo(c, t).start()
-
-            @pl.when(jnp.logical_not(there(offsets[c])))
-            def _(c=c, t=t):
-                got[c][t][...] = jnp.zeros(got[c][t].shape, got[c][t].dtype)
-                if c in (low, high):
-                    rim[c - low, t] = jnp.zeros(rim.shape[2:], rim.dtype)
+    stages = [(t, c) for group in (far, (low, high)) for t in range(tiles) for c in group]
+    for t, c in stages:
+        for slot in range(CAP):
+            pack[c, t, slot] = kv[t, picks[c][slot]]
+
+        @pl.when(there(offsets[c]))
+        def _(c=c, t=t):
+            if c in (low, high) and t > 0:
+                edge(c - low, t).start()
+            halo(c, t).start()
+
+        @pl.when(jnp.logical_not(there(offsets[c])))
+        def _(c=c, t=t):
+            got[c][t][...] = jnp.zeros(got[c][t].shape, got[c][t].dtype)
+            if c in (low, high):
+                rim[c - low, t] = jnp.zeros(rim.shape[2:], rim.dtype)
 
     def w_copy(step):
         peer = peers[step]
@@ -325,9 +335,15 @@
         out = pl.pallas_call(
             functools.partial(kernel, n_seq, n_head),
             out_shape=jax.ShapeDtypeStruct((bars, length, cols), jnp.bfloat16),
-            in_specs=[pl.BlockSpec(memory_space=pltpu.SMEM)] + [vmem] * 2 + [pl.BlockSpec(memory_space=pl.ANY)] * 4,
+            in_specs=[pl.BlockSpec(memory_space=pl.ANY)] * 7,
             out_specs=vmem,
-            scratch_shapes=[pltpu.VMEM((bars, length, width), jnp.bfloat16)] * 3
+            scratch_shapes=[
+                pltpu.SMEM(key_bars.shape, jnp.int32),
+                pltpu.VMEM((bars, length), jnp.int32),
+                pltpu.VMEM(mask_qkv.shape, jnp.bfloat16),
+                dma((3,)),
+            ]
+            + [pltpu.VMEM((bars, length, width), jnp.bfloat16)] * 3
             + [
                 dma((3, bars)),
                 pltpu.VMEM((tiles, bars, length, 2 * LANES), jnp.bfloat16),

time: 32.1 us -> 31.4 us (0.978)
  Pallas kernels: 30.1 us -> 29.4 us
    pallas_call x1, Pallas kernels: 30.1 us -> 29.4 us  [on_device(): pl.pallas_call(functools.partial(kernel, n_seq, n_head), out_shape=jax.Sh...]
where the time goes in v4:
time: 31.4 us; the launch traced here: 31.2 us
  Pallas kernels  29.4 us (94%)
  local copies, waits for them, and re-layouts  1.78 us (6%)
    pallas_call x1, Pallas kernels, on_device(): pl.pallas_call(functools.partial(kernel, n_seq, n_head), out_shape=jax.Sh...  29.4 us
    unnamed x1, local copies, waits for them, and re-layouts  1.78 us

profile of v4, /device:TPU:25, one launch (start us, length us, event | category | flops | bytes accessed | tf_op | source)
XLA Modules:
  0.0 31.2 jit_solution(11255149840743504238)
XLA Ops:
  0.0 29.4 %bar_attention.1 = bf16[4,128,384]{2,1,0:T(8,128)(2,1)} custom-call(s32[4,4]{1,0:T(4,128)} %bars_hbm.1, s32[4,128]{1,0:T(4,128)} %bitcast.9, bf16[3,256]{1,0:T(4,128)(2,1)} %mask_hbm.1, bf16[4,128,256]{2,1,0:T(8,128)(2,1)} %bitcast.6, bf16[4,128,256]{2,1,0:T(8,128)(2,1)} %bitcast.7, bf16[4,128,256]{2,1,0:T(8,128)(2,1)} %bitcast.8, bf16[256,1536]{1,0:T(8,128)(2,1)} %w_ref.1), custom_call_target="tpu_custom_call" | custom-call | tf_op jit(solution)/shard_map/bar_attention/pallas_call | solution.py:335
  29.4 1.8 %copy.9 = bf16[512,384]{1,0:T(8,128)(2,1)} copy(bf16[512,384]{1,0:T(8,128)(2,1)} %bitcast.5) | data formatting | bytes 786432
